TPU v7x, 32 devices: a whole 2x2x4 slice. The times are simulated.
32 devices in a mesh: energy: 2 (over y), slab: 16 (over z, x, core).
Axes of the slice: x: 2, y: 2, z: 4, core: 2. Of those that a mesh axis runs over, the one named last changes fastest.
Arguments:
- slab_green: bfloat16 [2, 128, 128, 128], P(None, ('energy', 'slab')), parts along dimension 1, may hold values from -1 to 1, as said below
- coupling: bfloat16 [2, 128, 128, 128], P(None, ('energy', 'slab')), parts along dimension 1, may hold values from -40 to 40
- left_lead_surface: bfloat16 [4, 128, 128], P('energy'), parts along dimension 0, may hold values from -8 to 8, as said below
- sigma_right: bfloat16 [4, 128, 128], P('energy'), parts along dimension 0, may hold values from -120 to 120, as said below
Outputs:
- green_diagonal: float32 [2, 128, 128, 128], P(None, ('energy', 'slab')), parts along dimension 1
There are 2 independent parts, one for each index of `energy`. A program takes and returns all parts, laid end to end along the dimension named above; each array names one. Nothing has to cross between parts.
Inputs may be any that keep to these rules, and one draw needn't show every extreme that they name: Each block of slab_green, both parts, equals its own transpose. `left_lead_surface`: both parts equal their own transposes. `sigma_right`: both parts equal their own transposes.
All inputs are finite; a program needn't handle non-finite values.
Results may differ from a plain program's by a relative error of at most 0.035.
Values may be sent and summed in bfloat16 or wider, within the bound.
A program may use at most 128 MiB of HBM per device.

v0:
```python
import functools

import jax
import jax.numpy as jnp
from jax import lax
from jax.experimental import pallas as pl
from jax.experimental.pallas import tpu as pltpu
from jax.sharding import PartitionSpec as P

MESH = pl.DeviceIdType.MESH
BF = jnp.bfloat16
F32 = jnp.float32


def wide(value):
    return jnp.concatenate([value[0], value[1]], axis=1)


def halves(out):
    width = out.shape[1] // 2
    return out[:, :width], out[:, width:]


def low(value):
    return value[0].astype(BF), value[1].astype(BF)


def plus(a, b):
    return a[0] + b[0], a[1] + b[1]


def times(rows, right):
    weights = jnp.concatenate(
        [wide(right), jnp.concatenate([-right[1], right[0]], axis=1)], axis=0
    )
    return jnp.dot(rows, weights, preferred_element_type=F32)


def times_transpose(rows, right):
    weights = jnp.concatenate(
        [
            jnp.concatenate([right[0], -right[1]], axis=1),
            jnp.concatenate([right[1], right[0]], axis=1),
        ],
        axis=0,
    )
    return lax.dot_general(rows, weights, (((1,), (1,)), ((), ())), preferred_element_type=F32)


def product(a, b):
    return low(halves(times(wide(a), b)))


def sandwich(factor, middle):
    inner = times(wide(factor), low(middle)).astype(BF)
    return halves(times_transpose(inner, factor))


def get(ref, *index):
    return ref[(*index, 0)], ref[(*index, 1)]


def put(ref, value, *index):
    ref[(*index, 0)] = value[0].astype(ref.dtype)
    ref[(*index, 1)] = value[1].astype(ref.dtype)


def kernel(
    rounds,
    green_hbm,
    link_hbm,
    lead_hbm,
    sigma_hbm,
    out,
    green,
    link,
    lead,
    sigma,
    own,
    pair,
    given,
    board,
    factors,
    base,
    inbox,
    outbox,
    ends,
    send_sem,
    recv_sem,
    load_sem,
):
    loads = [
        pltpu.make_async_copy(source, target, load_sem.at[k])
        for k, (source, target) in enumerate(
            [(green_hbm, green), (link_hbm, link), (lead_hbm, lead), (sigma_hbm, sigma)]
        )
    ]
    for load in loads:
        load.start()
    layers, width = green.shape[1], green.shape[2]
    energy, me = lax.axis_index("energy"), lax.axis_index("slab")
    role, chip = me % 2, me // 2
    mate = me + 1 - 2 * role
    bit = chip % 2
    side = (bit + role) % 2
    pal = me + (1 - 2 * bit) * 2
    steps = rounds - 1
    spot = chip // 2
    place = spot + role * (2**steps - 1 - 2 * spot)
    stride = (1 - 2 * role) * 4
    lows = [place // 2 ** (k + 1) * 2 ** (k + 1) for k in range(steps)]
    gives = [place == lows[k] + 2**k - 1 for k in range(steps)]
    takes = [(place // 2**k) % 2 == 1 for k in range(steps)]
    givers = [me + stride * (lows[k] + 2**k - 1 - place) for k in range(steps)]

    barrier = pltpu.get_barrier_semaphore()

    def greet(other):
        pl.semaphore_signal(barrier, inc=1, device_id=(energy, other), device_id_type=MESH)

    expected = 2
    greet(mate)
    greet(pal)
    for k in range(steps):
        expected = expected + jnp.where(gives[k], 2**k, 0) + jnp.where(takes[k], 1, 0)

        @pl.when(gives[k])
        def _():
            for d in range(2**k):
                greet(me + stride * (1 + d))

        @pl.when(takes[k])
        def _():
            greet(givers[k])

    def remote(source, target, other, sender, receiver):
        return pltpu.make_async_remote_copy(
            src_ref=source,
            dst_ref=target,
            send_sem=send_sem.at[sender],
            recv_sem=recv_sem.at[receiver],
            device_id=(energy, other),
            device_id_type=MESH,
        )

    zeros = jnp.zeros((width, width), BF)
    for k in range(steps):

        @pl.when(jnp.logical_not(takes[k]))
        def _():
            put(inbox, (zeros, zeros), k, 1)

        @pl.when(jnp.logical_or(jnp.logical_not(takes[k]), lows[k] == 0))
        def _():
            put(inbox, (zeros, zeros), k, 0)

    for load in loads[:2]:
        load.wait()
    g = [(green[0, i], green[1, i]) for i in range(layers)]
    c = [(link[0, i], link[1, i]) for i in range(layers)]
    ahead = [low(halves(times_transpose(wide(g[i]), c[i]))) for i in range(layers)]
    back = [product(c[i], g[i]) for i in range(layers)]
    hop = [halves(times_transpose(wide(back[i]), c[i])) for i in range(layers)]

    def merged(first, second):
        return (
            product(second[0], first[0]),
            plus(sandwich(second[0], first[1]), second[1]),
        )

    def whole(items):
        while len(items) > 1:
            rest = items[len(items) // 2 * 2 :]
            items = [merged(*items[k : k + 2]) for k in range(0, len(items) - 1, 2)] + rest
        return items[0]

    up = [(ahead[i], g[i]) for i in range(layers)]
    down = [(back[i], hop[i]) for i in reversed(range(layers))]
    up_total, down_total = whole(up), whole(down)

    put(own, up_total[0], role, 0)
    put(own, up_total[1], role, 1)
    put(own, down_total[0], 1 - role, 0)
    put(own, down_total[1], 1 - role, 1)
    pl.semaphore_wait(barrier, expected)
    swap = remote(own.at[1], pair, mate, 0, 0)
    swap.start()

    up_part, down_part = [up[0]], [down[0]]
    for i in range(1, layers):
        up_part.append(merged(up_part[-1], up[i]) if i + 1 < layers else up_total)
        if i + 1 < layers:
            down_part.append(merged(down_part[-1], down[i]))
    for i in range(layers):
        m_part, s_part = up_part[i]
        put(factors, m_part, role, i)
        if i + 1 < layers:
            m_rest, s_rest = down_part[layers - 2 - i]
            put(factors, product(g[i], m_rest), 1 - role, i)
            put(base, plus(s_part, sandwich(g[i], s_rest)), i)
        else:
            put(factors, g[i], 1 - role, i)
            put(base, s_part, i)

    for load in loads[2:]:
        load.wait()
    swap.wait_recv()
    last = 2 + 2 * steps
    hint = remote(own.at[0], given, mate, 2 * 2**steps + 1, last + 1)
    hint.start()
    total = merged((get(own, 0, 0), get(own, 0, 1)), (get(pair, 0), get(pair, 1)))
    forward = role == 0
    start = (
        jnp.where(forward, lead[0], sigma[0]),
        jnp.where(forward, lead[1], sigma[1]),
    )
    row = lax.broadcasted_iota(jnp.int32, (width, width), 0)
    column = lax.broadcasted_iota(jnp.int32, (width, width), 1)
    square = jnp.where(row == column, 1.0, 0.0).astype(BF)

    def wider(value):
        return value[0].astype(F32), value[1].astype(F32)

    def pick(test, a, b):
        return jnp.where(test, a[0], b[0]), jnp.where(test, a[1], b[1])

    def choose(test, a, b):
        return pick(test, a[0], b[0]), pick(test, a[1], b[1])

    put(board, total[0], side, 0)
    put(board, total[1], side, 1)
    cross = remote(board.at[side], board.at[side], pal, 1, 1)
    cross.start()
    cross.wait_recv()
    first = (get(board, 0, 0), wider(get(board, 0, 1)))
    second = (get(board, 1, 0), wider(get(board, 1, 1)))
    total = merged(first, second)
    none = (zeros, zeros)
    head = place == 0

    def settled(value):
        return pick(head, none, value[0]), pick(
            head, plus(sandwich(value[0], start), value[1]), value[1]
        )

    total = settled(total)

    def deliveries(k):
        found = []
        for d in range(2**k):
            other = me + stride * (1 + d)
            at = 2 + 2 * (2**k - 1 + d)
            found.append(
                (
                    remote(outbox.at[k, 1], inbox.at[k, 1], other, at, 2 + 2 * k),
                    remote(outbox.at[k, 0], inbox.at[k, 0], other, at + 1, 3 + 2 * k),
                )
            )
        return found

    def send(k):
        @pl.when(gives[k])
        def _():
            put(outbox, total[1], k, 1)
            put(outbox, total[0], k, 0)
            sent = deliveries(k)
            for constant, _ in reversed(sent):
                constant.start()
            if k + 1 < steps:

                @pl.when(lows[k] != 0)
                def _():
                    for _, linear in sent:
                        linear.start()

    def receive(k):
        @pl.when(takes[k])
        def _():
            constant, linear = deliveries(k)[0]
            constant.wait_recv()
            if k + 1 < steps:

                @pl.when(lows[k] != 0)
                def _():
                    linear.wait_recv()

        return get(inbox, k, 0), wider(get(inbox, k, 1))

    def finish(k):
        @pl.when(gives[k])
        def _():
            sent = deliveries(k)
            for constant, _ in sent:
                constant.wait_send()
            if k + 1 < steps:

                @pl.when(lows[k] != 0)
                def _():
                    for _, linear in sent:
                        linear.wait_send()

    if steps:
        send(0)
    before = settled(
        (
            pick(side == 1, first[0], (square, zeros)),
            pick(side == 1, first[1], wider(none)),
        )
    )
    hint.wait_recv()
    for i in range(layers):
        factor = get(factors, 1, i)
        put(base, plus(get(base, i), sandwich(factor, get(given, 1))), i)
        put(factors, product(factor, get(given, 0)), 1, i)
    for k in range(steps):
        got = receive(k)
        if k + 1 < steps:
            total = choose(takes[k], merged(got, total), total)
            send(k + 1)
        before = choose(takes[k], merged(got, before), before)
    entering = before[1]
    put(ends, entering, role)
    share = remote(ends.at[role], ends.at[role], mate, 2 * 2**steps, last)
    share.start()

    def spread(k, middle):
        rows = jnp.concatenate([wide(get(factors, k, i)) for i in range(layers)], axis=0)
        inner = times(rows, low(middle)).astype(BF)
        return [
            halves(times_transpose(inner[i * width : (i + 1) * width], get(factors, k, i)))
            for i in range(layers)
        ]

    mine = spread(0, entering)
    for i in range(layers):
        put(base, plus(get(base, i), mine[i]), i)
    share.wait_recv()
    theirs = spread(1, get(ends, 1 - role))
    for i in range(layers):
        value = plus(get(base, i), theirs[i])
        out[0, i] = value[0]
        out[1, i] = value[1]

    swap.wait_send()
    hint.wait_send()
    cross.wait_send()
    share.wait_send()
    for k in range(steps):
        finish(k)


def solution(mesh):
    peers = mesh.shape["slab"]
    rounds = (peers // 2).bit_length() - 1

    def local(slab_green, coupling, left_lead_surface, sigma_right):
        layers, width = slab_green.shape[1], slab_green.shape[2]
        vmem = pl.BlockSpec(memory_space=pltpu.VMEM)
        block = (2, width, width)
        return pl.pallas_call(
            functools.partial(kernel, rounds),
            out_shape=jax.ShapeDtypeStruct(slab_green.shape, F32),
            in_specs=[pl.BlockSpec(memory_space=pltpu.HBM)] * 4,
            out_specs=vmem,
            scratch_shapes=[
                pltpu.VMEM(slab_green.shape, BF),
                pltpu.VMEM(coupling.shape, BF),
                pltpu.VMEM(block, BF),
                pltpu.VMEM(block, BF),
                pltpu.VMEM((2, 2, *block), BF),
                pltpu.VMEM((2, *block), BF),
                pltpu.VMEM((2, *block), BF),
                pltpu.VMEM((2, 2, *block), BF),
                pltpu.VMEM((2, layers, *block), BF),
                pltpu.VMEM((layers, *block), F32),
                pltpu.VMEM((max(rounds - 1, 1), 2, *block), BF),
                pltpu.VMEM((max(rounds - 1, 1), 2, *block), BF),
                pltpu.VMEM((2, *block), BF),
                pltpu.SemaphoreType.DMA((2**rounds + 2,)),
                pltpu.SemaphoreType.DMA((2 * rounds + 2,)),
                pltpu.SemaphoreType.DMA((4,)),
            ],
            compiler_params=pltpu.CompilerParams(collective_id=0, has_side_effects=True, vmem_limit_bytes=16777216),
        )(*[pltpu.with_memory_space_constraint(a, pltpu.HBM) for a in (slab_green, coupling, left_lead_surface, sigma_right)])

    in_specs = (
        P(None, ("energy", "slab"), None, None),
        P(None, ("energy", "slab"), None, None),
        P("energy", None, None),
        P("energy", None, None),
    )
    out_specs = P(None, ("energy", "slab"), None, None)
    return jax.shard_map(local, mesh=mesh, in_specs=in_specs, out_specs=out_specs, check_vma=False)
```

profile of v0, /device:TPU:0, one launch (start us, length us, event | category | flops | bytes accessed | tf_op | source)
XLA Modules:
  0.0 21.0 jit_solution(1801112721195671466)
XLA Ops:
  0.0 20.2 %shard_map.46 = f32[2,4,128,128]{3,2,1,0:T(8,128)S(1)} custom-call(bf16[2,4,128,128]{3,2,1,0:T(8,128)(2,1)} %green_hbm.1, bf16[2,4,128,128]{3,2,1,0:T(8,128)(2,1)} %link_hbm.1, bf16[2,128,128]{2,1,0:T(8,128)(2,1)} %lead_hbm.1, bf16[2,128,128]{2,1,0:T(8,128)(2,1)} %sigma_hbm.1), custom_call_target="tpu_custom_call" | custom-call | tf_op jit(solution)/shard_map/pallas_call | solution.py:360
  20.2 0.8 %copy.6 = f32[2,4,128,128]{3,2,1,0:T(8,128)} copy(f32[2,4,128,128]{3,2,1,0:T(8,128)S(1)} %shard_map.46) | data formatting | bytes 1048576
where the time goes:
time: 21.2 us; the launch traced here: 21 us
  Pallas kernels  20.2 us (95%)
  local copies, waits for them, and re-layouts  0.8 us (4%)
    pallas_call x1, Pallas kernels, local(): pl.pallas_call(functools.partial(kernel, rounds), out_shape=jax.ShapeDtyp...  20.2 us
    unnamed x1, local copies, waits for them, and re-layouts  0.8 us

commit v1 on v0

v1 whole, which is shorter than its diff:
```python
import functools

import jax
import jax.numpy as jnp
from jax import lax
from jax.experimental import pallas as pl
from jax.experimental.pallas import tpu as pltpu
from jax.sharding import PartitionSpec as P

MESH = pl.DeviceIdType.MESH
BF = jnp.bfloat16
F32 = jnp.float32


def wide(value):
    return jnp.concatenate([value[0], value[1]], axis=1)


def halves(out):
    width = out.shape[1] // 2
    return out[:, :width], out[:, width:]


def low(value):
    return value[0].astype(BF), value[1].astype(BF)


def plus(a, b):
    return a[0] + b[0], a[1] + b[1]


def times(rows, right):
    weights = jnp.concatenate(
        [wide(right), jnp.concatenate([-right[1], right[0]], axis=1)], axis=0
    )
    return jnp.dot(rows, weights, preferred_element_type=F32)


def times_transpose(rows, right):
    weights = jnp.concatenate(
        [
            jnp.concatenate([right[0], -right[1]], axis=1),
            jnp.concatenate([right[1], right[0]], axis=1),
        ],
        axis=0,
    )
    return lax.dot_general(rows, weights, (((1,), (1,)), ((), ())), preferred_element_type=F32)


def product(a, b):
    return low(halves(times(wide(a), b)))


def sandwich(factor, middle):
    inner = times(wide(factor), low(middle)).astype(BF)
    return halves(times_transpose(inner, factor))


def get(ref, *index):
    return ref[(*index, 0)], ref[(*index, 1)]


def put(ref, value, *index):
    ref[(*index, 0)] = value[0].astype(ref.dtype)
    ref[(*index, 1)] = value[1].astype(ref.dtype)


def kernel(
    bits,
    near,
    green_hbm,
    link_hbm,
    lead_hbm,
    sigma_hbm,
    out,
    green,
    link,
    lead,
    sigma,
    own,
    pair,
    given,
    factors,
    base,
    mine,
    slots,
    relay,
    inbox,
    ends,
    post,
    late,
    send_sem,
    recv_sem,
    load_sem,
):
    loads = [
        pltpu.make_async_copy(source, target, load_sem.at[k])
        for k, (source, target) in enumerate(
            [(green_hbm, green), (link_hbm, link), (lead_hbm, lead), (sigma_hbm, sigma)]
        )
    ]
    for load in loads:
        load.start()
    layers, width = green.shape[1], green.shape[2]
    energy, me = lax.axis_index("energy"), lax.axis_index("slab")
    role, chip = me % 2, me // 2
    mate = me + 1 - 2 * role
    chips, half, group = 2**bits, 2 ** (bits - 1), 2**near
    place = chip + role * (chips - 1 - 2 * chip)
    stride = (1 - 2 * role) * 2
    spot = place % group
    head = place == 0
    middle = range(near, bits - 1)
    lows = {k: place // 2 ** (k + 1) * 2 ** (k + 1) for k in middle}
    gives = {k: place == lows[k] + 2**k - 1 for k in middle}
    takes = {k: (place // 2**k) % 2 == 1 for k in middle}
    gives_last = place == half - 1
    upper = chip // half
    giver = jnp.where(upper == 1, 2 * (half - 1), 2 * half + 1)
    slow = (1 - upper + role) % 2

    barrier = pltpu.get_barrier_semaphore()

    def greet(other):
        pl.semaphore_signal(barrier, inc=1, device_id=(energy, other), device_id_type=MESH)

    greet(mate)
    expected = 1 + (group - 1 - spot)
    for d in range(1, group):

        @pl.when(spot >= d)
        def _():
            greet(me - stride * d)

    for k in middle:
        expected = expected + jnp.where(gives[k], 2**k, 0)

        @pl.when(takes[k])
        def _():
            greet(me + stride * (lows[k] + 2**k - 1 - place))

    expected = expected + jnp.where(gives_last, 2 * half, 0)
    greet_last = jnp.logical_not(giver == me)

    @pl.when(greet_last)
    def _():
        greet(giver)

    def remote(source, target, other, sender, receiver):
        return pltpu.make_async_remote_copy(
            src_ref=source,
            dst_ref=target,
            send_sem=send_sem.at[sender],
            recv_sem=recv_sem.at[receiver],
            device_id=(energy, other),
            device_id_type=MESH,
        )

    row = lax.broadcasted_iota(jnp.int32, (width, width), 0)
    column = lax.broadcasted_iota(jnp.int32, (width, width), 1)
    zeros = jnp.zeros((width, width), BF)
    square = jnp.where(row == column, 1.0, 0.0).astype(BF)
    none = (zeros, zeros)
    linear, constant = pl.ds(0, 2 * width), pl.ds(2 * width, width + 16)

    def wider(value):
        return value[0].astype(F32), value[1].astype(F32)

    def pick(test, a, b):
        return jnp.where(test, a[0], b[0]), jnp.where(test, a[1], b[1])

    def put_linear(ref, value, *index):
        ref[(*index, pl.ds(0, width))] = value[0]
        ref[(*index, pl.ds(width, width))] = value[1]

    def put_packed(ref, value, at, *index):
        ref[(*index, pl.ds(at, width))] = jnp.where(row <= column, value[0], value[1]).astype(BF)
        diagonal = jnp.sum(jnp.where(row == column, value[1], 0.0), axis=0, keepdims=True)
        ref[(*index, pl.ds(at + width, 16))] = jnp.broadcast_to(diagonal, (16, width)).astype(BF)

    def get_packed(ref, at, *index):
        mixed = ref[(*index, pl.ds(at, width))]
        flipped = mixed.T.astype(F32)
        mixed = mixed.astype(F32)
        diagonal = ref[(*index, pl.ds(at + width, 16))].astype(F32)[0:1]
        return (
            jnp.where(row <= column, mixed, flipped),
            jnp.where(row > column, mixed, jnp.where(row == column, diagonal, flipped)),
        )

    def get_map(ref, *index):
        first = (ref[(*index, pl.ds(0, width))], ref[(*index, pl.ds(width, width))])
        return first, get_packed(ref, 2 * width, *index)

    def put_map(ref, value, *index):
        put_linear(ref, value[0], *index)
        put_packed(ref, value[1], 2 * width, *index)

    blank = jnp.zeros((width + 16, width), BF)
    for d in range(1, group):

        @pl.when(spot < d)
        def _():
            put_linear(slots, (square, zeros), d - 1)
            slots[d - 1, constant] = blank

        @pl.when(place == d)
        def _():
            put_linear(slots, none, d - 1)

    for k in middle:

        @pl.when(jnp.logical_not(takes[k]))
        def _():
            put_linear(inbox, (square, zeros), k - near)
            inbox[k - near, constant] = blank

        @pl.when(jnp.logical_and(takes[k], lows[k] == 0))
        def _():
            put_linear(inbox, none, k - near)

    for load in loads[:2]:
        load.wait()

    def merged(first, second):
        return (
            product(second[0], first[0]),
            plus(sandwich(second[0], first[1]), second[1]),
        )

    def whole(items):
        while len(items) > 1:
            rest = items[len(items) // 2 * 2 :]
            items = [merged(*items[k : k + 2]) for k in range(0, len(items) - 1, 2)] + rest
        return items[0]

    def blocks():
        return (
            [(green[0, i], green[1, i]) for i in range(layers)],
            [(link[0, i], link[1, i]) for i in range(layers)],
        )

    def upward():
        g, c = blocks()
        return [(low(halves(times_transpose(wide(g[i]), c[i]))), g[i]) for i in range(layers)]

    def downward():
        g, c = blocks()
        back = [product(c[i], g[i]) for i in range(layers)]
        return [(back[i], halves(times_transpose(wide(back[i]), c[i]))) for i in range(layers)]

    def total_to(at, up):
        def _():
            value = whole(upward()) if up else whole(downward()[::-1])
            put(own, value[0], at, 0)
            put(own, value[1], at, 1)

        return _

    pl.when(role == 0)(total_to(1, False))
    pl.when(role == 1)(total_to(1, True))
    pl.semaphore_wait(barrier, expected)
    swap = remote(own.at[1], pair, mate, 0, 0)
    swap.start()
    pl.when(role == 0)(total_to(0, True))
    pl.when(role == 1)(total_to(0, False))
    hint = remote(own.at[0], given, mate, 1, 1)
    hint.start()

    for load in loads[2:]:
        load.wait()
    forward = role == 0
    start = (
        jnp.where(forward, lead[0], sigma[0]),
        jnp.where(forward, lead[1], sigma[1]),
    )
    first = (get(own, 0, 0), wider(get(own, 0, 1)))
    first = (first[0], pick(head, plus(sandwich(first[0], start), first[1]), first[1]))
    swap.wait_recv()
    total = merged(first, (get(pair, 0), wider(get(pair, 1))))
    total = (pick(head, none, total[0]), total[1])
    put_map(mine, total)

    def neighbour(d, whole_map):
        part = pl.ds(0, 3 * width + 16) if whole_map else constant
        return remote(mine.at[part], slots.at[d - 1, part], me + stride * d, 2 + d, 2 + d)

    def for_kinds(d, sender, act):
        test = spot + d < group if sender else spot >= d
        at_head = head if sender else place == d
        pl.when(jnp.logical_and(test, at_head))(lambda: act(neighbour(d, False)))
        pl.when(jnp.logical_and(test, jnp.logical_not(at_head)))(lambda: act(neighbour(d, True)))

    for d in reversed(range(1, group)):
        for_kinds(d, True, lambda copy: copy.start())

    g = blocks()[0]
    up, down = upward(), downward()[::-1]
    up_part, down_part = [up[0]], [down[0]]
    for i in range(1, layers):
        up_part.append(merged(up_part[-1], up[i]))
        if i + 1 < layers:
            down_part.append(merged(down_part[-1], down[i]))
    for i in range(layers):
        m_part, s_part = up_part[i]
        put(factors, m_part, role, i)
        if i + 1 < layers:
            m_rest, s_rest = down_part[layers - 2 - i]
            put(factors, product(g[i], m_rest), 1 - role, i)
            put(base, plus(s_part, sandwich(g[i], s_rest)), i)
        else:
            put(factors, g[i], 1 - role, i)
            put(base, s_part, i)
    hint.wait_recv()
    for i in range(layers):
        factor = get(factors, 1, i)
        put(base, plus(get(base, i), sandwich(factor, get(given, 1))), i)
        put(factors, product(factor, get(given, 0)), 1, i)

    for d in reversed(range(1, group)):
        for_kinds(d, False, lambda copy: copy.wait_recv())
    arrived = [get_map(slots, d - 1) for d in reversed(range(1, group))]
    if arrived:
        lower = arrived[:-1] and [whole(arrived[:-1])]
        before = whole(lower + arrived[-1:])
        total = whole(lower + [merged(arrived[-1], total)])
    else:
        before = ((square, zeros), wider(none))
    before = (pick(head, none, before[0]), pick(head, wider(start), before[1]))

    def deliveries(k, whole_map):
        part = pl.ds(0, 3 * width + 16) if whole_map else constant
        at = 2 + group + 2 ** k - 2**near
        return [
            remote(relay.at[k - near, part], inbox.at[k - near, part], me + stride * (1 + d), at + d, 2 + group + k - near)
            for d in range(2**k)
        ]

    for k in middle:

        @pl.when(gives[k])
        def _():
            put_map(relay, total, k - near)

        for whole_map in (False, True):

            @pl.when(jnp.logical_and(gives[k], (lows[k] != 0) == whole_map))
            def _():
                for copy in reversed(deliveries(k, whole_map)):
                    copy.start()

            @pl.when(jnp.logical_and(takes[k], (lows[k] != 0) == whole_map))
            def _():
                deliveries(k, whole_map)[0].wait_recv()

        got = get_map(inbox, k - near)
        total = merged(got, total)
        before = merged(got, before)

    last = 2 + group + half - 2**near
    last_recv = 2 + group + len(middle)

    def final(d, twin):
        other = me + stride * (1 + d)
        other = other + 1 - 2 * role if twin else other
        return remote(post, late, other, last + 2 * d + twin, last_recv)

    @pl.when(gives_last)
    def _():
        put_packed(post, total[1], 0)
        for d in reversed(range(half)):
            final(d, 0).start()
            final(d, 1).start()

    put(ends, before[0], 0, 0)
    put(ends, before[1], 0, 1)
    share = remote(ends.at[0], ends.at[1], mate, 2, 2)
    share.start()

    def add(k):
        rows = jnp.concatenate([wide(get(factors, k, i)) for i in range(layers)], axis=0)
        inner = times(rows, get(ends, k, 1)).astype(BF)
        for i in range(layers):
            term = halves(times_transpose(inner[i * width : (i + 1) * width], get(factors, k, i)))
            put(base, plus(get(base, i), term), i)

    add(0)
    share.wait_recv()
    add(1)
    edge = get(ends, slow, 0)
    rows = jnp.concatenate([wide(get(factors, slow, i)) for i in range(layers)], axis=0)
    rows = times(rows, edge).astype(BF)
    final(0, 0).wait_recv()
    state = low(get_packed(late, 0))
    inner = times(rows, state).astype(BF)
    for i in range(layers):
        part = slice(i * width, (i + 1) * width)
        value = plus(get(base, i), halves(times_transpose(inner[part], halves(rows[part]))))
        out[0, i] = value[0]
        out[1, i] = value[1]

    swap.wait_send()
    hint.wait_send()
    share.wait_send()
    for d in range(1, group):
        for_kinds(d, True, lambda copy: copy.wait_send())
    for k in middle:
        for whole_map in (False, True):

            @pl.when(jnp.logical_and(gives[k], (lows[k] != 0) == whole_map))
            def _():
                for copy in deliveries(k, whole_map):
                    copy.wait_send()

    @pl.when(gives_last)
    def _():
        for d in range(half):
            final(d, 0).wait_send()
            final(d, 1).wait_send()


def solution(mesh):
    peers = mesh.shape["slab"]
    bits = (peers // 2).bit_length() - 1
    near = min(2, bits - 1)
    group, half, hops = 2**near, 2 ** (bits - 1), bits - 1 - near

    def local(slab_green, coupling, left_lead_surface, sigma_right):
        layers, width = slab_green.shape[1], slab_green.shape[2]
        vmem = pl.BlockSpec(memory_space=pltpu.VMEM)
        block = (2, width, width)
        packed, chart = (width + 16, width), (3 * width + 16, width)
        return pl.pallas_call(
            functools.partial(kernel, bits, near),
            out_shape=jax.ShapeDtypeStruct(slab_green.shape, F32),
            in_specs=[pl.BlockSpec(memory_space=pltpu.HBM)] * 4,
            out_specs=vmem,
            scratch_shapes=[
                pltpu.VMEM(slab_green.shape, BF),
                pltpu.VMEM(coupling.shape, BF),
                pltpu.VMEM(block, BF),
                pltpu.VMEM(block, BF),
                pltpu.VMEM((2, 2, *block), BF),
                pltpu.VMEM((2, *block), BF),
                pltpu.VMEM((2, *block), BF),
                pltpu.VMEM((2, layers, *block), BF),
                pltpu.VMEM((layers, *block), F32),
                pltpu.VMEM(chart, BF),
                pltpu.VMEM((max(group - 1, 1), *chart), BF),
                pltpu.VMEM((max(hops, 1), *chart), BF),
                pltpu.VMEM((max(hops, 1), *chart), BF),
                pltpu.VMEM((2, 2, *block), BF),
                pltpu.VMEM(packed, BF),
                pltpu.VMEM(packed, BF),
                pltpu.SemaphoreType.DMA((2 + group + half - group + 2 * half,)),
                pltpu.SemaphoreType.DMA((3 + group + hops,)),
                pltpu.SemaphoreType.DMA((4,)),
            ],
            compiler_params=pltpu.CompilerParams(collective_id=0, has_side_effects=True, vmem_limit_bytes=16777216),
        )(*[pltpu.with_memory_space_constraint(a, pltpu.HBM) for a in (slab_green, coupling, left_lead_surface, sigma_right)])

    in_specs = (
        P(None, ("energy", "slab"), None, None),
        P(None, ("energy", "slab"), None, None),
        P("energy", None, None),
        P("energy", None, None),
    )
    out_specs = P(None, ("energy", "slab"), None, None)
    return jax.shard_map(local, mesh=mesh, in_specs=in_specs, out_specs=out_specs, check_vma=False)
```

time: 21.2 us -> 15.8 us (0.75)
  Pallas kernels: 20.2 us -> 14.7 us
    pallas_call x1, Pallas kernels: 20.2 us -> 14.7 us  [local(): pl.pallas_call(functools.partial(kernel, bits, near), out_shape=jax.Shape...]
where the time goes in v1:
time: 15.8 us; the launch traced here: 15.5 us
  Pallas kernels  14.7 us (93%)
  local copies, waits for them, and re-layouts  0.8 us (5%)
    pallas_call x1, Pallas kernels, local(): pl.pallas_call(functools.partial(kernel, bits, near), out_shape=jax.Shape...  14.7 us
    unnamed x1, local copies, waits for them, and re-layouts  0.8 us

profile of v1, /device:TPU:0, one launch (start us, length us, event | category | flops | bytes accessed | tf_op | source)
XLA Modules:
  0.0 15.5 jit_solution(8793533394869333418)
XLA Ops:
  0.0 14.7 %shard_map.46 = f32[2,4,128,128]{3,2,1,0:T(8,128)S(1)} custom-call(bf16[2,4,128,128]{3,2,1,0:T(8,128)(2,1)} %green_hbm.1, bf16[2,4,128,128]{3,2,1,0:T(8,128)(2,1)} %link_hbm.1, bf16[2,128,128]{2,1,0:T(8,128)(2,1)} %lead_hbm.1, bf16[2,128,128]{2,1,0:T(8,128)(2,1)} %sigma_hbm.1), custom_call_target="tpu_custom_call" | custom-call | tf_op jit(solution)/shard_map/pallas_call | solution.py:433
  14.7 0.8 %copy.6 = f32[2,4,128,128]{3,2,1,0:T(8,128)} copy(f32[2,4,128,128]{3,2,1,0:T(8,128)S(1)} %shard_map.46) | data formatting | bytes 1048576

commit v2 on v1

--- a/solution.py
+++ b/solution.py
@@ -92,6 +92,7 @@
     send_sem,
     recv_sem,
     load_sem,
+    met,
 ):
     loads = [
         pltpu.make_async_copy(source, target, load_sem.at[k])
@@ -124,27 +125,40 @@
     def greet(other):
         pl.semaphore_signal(barrier, inc=1, device_id=(energy, other), device_id_type=MESH)
 
-    greet(mate)
-    expected = 1 + (group - 1 - spot)
+    def far_greet(other):
+        greet(other // 2 * 2 + 1)
+
+    def receivers(place):
+        found = group - 1 - place % group + jnp.where(place == half - 1, 2 * half, 0)
+        for k in middle:
+            found = found + jnp.where(place % 2 ** (k + 1) == 2**k - 1, 2**k, 0)
+        return found
+
     for d in range(1, group):
 
         @pl.when(spot >= d)
         def _():
-            greet(me - stride * d)
+            far_greet(me - stride * d)
 
     for k in middle:
-        expected = expected + jnp.where(gives[k], 2**k, 0)
 
         @pl.when(takes[k])
         def _():
-            greet(me + stride * (lows[k] + 2**k - 1 - place))
-
-    expected = expected + jnp.where(gives_last, 2 * half, 0)
-    greet_last = jnp.logical_not(giver == me)
-
-    @pl.when(greet_last)
-    def _():
-        greet(giver)
+            far_greet(me + stride * (lows[k] + 2**k - 1 - place))
+
+    far_greet(giver)
+
+    def tell(at):
+        pl.semaphore_signal(met.at[at], inc=1, device_id=(energy, mate), device_id_type=MESH)
+
+    @pl.when(role == 1)
+    def _():
+        greet(mate)
+
+    @pl.when(role == 0)
+    def _():
+        pl.semaphore_wait(barrier, 1)
+        tell(0)
 
     def remote(source, target, other, sender, receiver):
         return pltpu.make_async_remote_copy(
@@ -259,7 +273,11 @@
 
     pl.when(role == 0)(total_to(1, False))
     pl.when(role == 1)(total_to(1, True))
-    pl.semaphore_wait(barrier, expected)
+
+    @pl.when(role == 1)
+    def _():
+        pl.semaphore_wait(met.at[0], 1)
+
     swap = remote(own.at[1], pair, mate, 0, 0)
     swap.start()
     pl.when(role == 0)(total_to(0, True))
@@ -277,9 +295,19 @@
     first = (get(own, 0, 0), wider(get(own, 0, 1)))
     first = (first[0], pick(head, plus(sandwich(first[0], start), first[1]), first[1]))
     swap.wait_recv()
+
+    @pl.when(role == 1)
+    def _():
+        pl.semaphore_wait(barrier, receivers(chip) + receivers(chips - 1 - chip))
+        tell(1)
+
     total = merged(first, (get(pair, 0), wider(get(pair, 1))))
     total = (pick(head, none, total[0]), total[1])
     put_map(mine, total)
+
+    @pl.when(role == 0)
+    def _():
+        pl.semaphore_wait(met.at[1], 1)
 
     def neighbour(d, whole_map):
         part = pl.ds(0, 3 * width + 16) if whole_map else constant
@@ -455,6 +483,7 @@
                 pltpu.SemaphoreType.DMA((2 + group + half - group + 2 * half,)),
                 pltpu.SemaphoreType.DMA((3 + group + hops,)),
                 pltpu.SemaphoreType.DMA((4,)),
+                pltpu.SemaphoreType.REGULAR((2,)),
             ],
             compiler_params=pltpu.CompilerParams(collective_id=0, has_side_effects=True, vmem_limit_bytes=16777216),
         )(*[pltpu.with_memory_space_constraint(a, pltpu.HBM) for a in (slab_green, coupling, left_lead_surface, sigma_right)])

time: 15.8 us -> 15.7 us (level)
  no operation moved by 1% of the time
where the time goes in v2:
time: 15.7 us; the launch traced here: 15.6 us
  Pallas kernels  14.8 us (94%)
  local copies, waits for them, and re-layouts  0.8 us (5%)
    pallas_call x1, Pallas kernels, local(): pl.pallas_call(functools.partial(kernel, bits, near), out_shape=jax.Shape...  14.8 us
    unnamed x1, local copies, waits for them, and re-layouts  0.8 us

profile of v2, /device:TPU:0, one launch (start us, length us, event | category | flops | bytes accessed | tf_op | source)
XLA Modules:
  0.0 15.6 jit_solution(164176022286091364)
XLA Ops:
  0.0 14.8 %shard_map.46 = f32[2,4,128,128]{3,2,1,0:T(8,128)S(1)} custom-call(bf16[2,4,128,128]{3,2,1,0:T(8,128)(2,1)} %green_hbm.1, bf16[2,4,128,128]{3,2,1,0:T(8,128)(2,1)} %link_hbm.1, bf16[2,128,128]{2,1,0:T(8,128)(2,1)} %lead_hbm.1, bf16[2,128,128]{2,1,0:T(8,128)(2,1)} %sigma_hbm.1), custom_call_target="tpu_custom_call" | custom-call | tf_op jit(solution)/shard_map/pallas_call | solution.py:461
  14.8 0.8 %copy.6 = f32[2,4,128,128]{3,2,1,0:T(8,128)} copy(f32[2,4,128,128]{3,2,1,0:T(8,128)S(1)} %shard_map.46) | data formatting | bytes 1048576

commit v3 on v2

--- a/solution.py
+++ b/solution.py
@@ -82,7 +82,6 @@
     given,
     factors,
     base,
-    mine,
     slots,
     relay,
     inbox,
@@ -107,6 +106,7 @@
     role, chip = me % 2, me // 2
     mate = me + 1 - 2 * role
     chips, half, group = 2**bits, 2 ** (bits - 1), 2**near
+    duo = min(2, group)
     place = chip + role * (chips - 1 - 2 * chip)
     stride = (1 - 2 * role) * 2
     spot = place % group
@@ -115,9 +115,10 @@
     lows = {k: place // 2 ** (k + 1) * 2 ** (k + 1) for k in middle}
     gives = {k: place == lows[k] + 2**k - 1 for k in middle}
     takes = {k: (place // 2**k) % 2 == 1 for k in middle}
-    gives_last = place == half - 1
+    gives_last = place // duo == half // duo - 1
     upper = chip // half
-    giver = jnp.where(upper == 1, 2 * (half - 1), 2 * half + 1)
+    there = half - duo + jnp.where(upper == 1, chip, chips - 1 - chip) % duo
+    giver = jnp.where(upper == 1, there, chips - 1 - there) * 2
     slow = (1 - upper + role) % 2
 
     barrier = pltpu.get_barrier_semaphore()
@@ -129,16 +130,25 @@
         greet(other // 2 * 2 + 1)
 
     def receivers(place):
-        found = group - 1 - place % group + jnp.where(place == half - 1, 2 * half, 0)
+        found = group - 1 - place % group + jnp.where(place // duo == half // duo - 1, 2 * (half // duo), 0)
+        if duo > 1:
+            found = found + jnp.where(place % group == group - 1, 1, 0)
         for k in middle:
             found = found + jnp.where(place % 2 ** (k + 1) == 2**k - 1, 2**k, 0)
         return found
 
-    for d in range(1, group):
-
-        @pl.when(spot >= d)
-        def _():
-            far_greet(me - stride * d)
+    def sources():
+        for p in range(group):
+            test = p < spot
+            if duo > 1 and p == group - 1:
+                test = spot == group - 2
+            yield p, test, place - spot + p == 0
+
+    for p, test, _ in sources():
+
+        @pl.when(test)
+        def _():
+            far_greet(me + stride * (p - spot))
 
     for k in middle:
 
@@ -211,16 +221,16 @@
         put_packed(ref, value[1], 2 * width, *index)
 
     blank = jnp.zeros((width + 16, width), BF)
-    for d in range(1, group):
-
-        @pl.when(spot < d)
-        def _():
-            put_linear(slots, (square, zeros), d - 1)
-            slots[d - 1, constant] = blank
-
-        @pl.when(place == d)
-        def _():
-            put_linear(slots, none, d - 1)
+    for p, test, first in sources():
+
+        @pl.when(jnp.logical_not(jnp.logical_or(test, spot == p)))
+        def _():
+            put_linear(slots, (square, zeros), p)
+            slots[p, constant] = blank
+
+        @pl.when(jnp.logical_and(test, first))
+        def _():
+            put_linear(slots, none, p)
 
     for k in middle:
 
@@ -263,64 +273,65 @@
         back = [product(c[i], g[i]) for i in range(layers)]
         return [(back[i], halves(times_transpose(wide(back[i]), c[i]))) for i in range(layers)]
 
-    def total_to(at, up):
-        def _():
-            value = whole(upward()) if up else whole(downward()[::-1])
-            put(own, value[0], at, 0)
-            put(own, value[1], at, 1)
-
-        return _
-
-    pl.when(role == 0)(total_to(1, False))
-    pl.when(role == 1)(total_to(1, True))
+    def keep(at, value):
+        put(own, value[0], at, 0)
+        put(own, value[1], at, 1)
+
+    def neighbour(source, target, whole_map):
+        part = pl.ds(0, 3 * width + 16) if whole_map else constant
+        return remote(
+            slots.at[source, part], slots.at[source, part], me + stride * (target - spot), 3 + target, 3 + source
+        )
+
+    def by_kind(test, first, source, target, act):
+        pl.when(jnp.logical_and(test, first))(lambda: act(neighbour(source, target, False)))
+        pl.when(jnp.logical_and(test, jnp.logical_not(first)))(lambda: act(neighbour(source, target, True)))
+
+    def for_targets(act):
+        for p in reversed(range(group)):
+            test = spot < p
+            if duo > 1 and p == group - 2:
+                test = jnp.logical_or(test, spot == group - 1)
+            by_kind(test, head, spot, p, act)
+
+    forward = role == 0
+    swap = remote(own.at[1], pair, mate, 0, 0)
+
+    def advance():
+        start = (
+            jnp.where(forward, lead[0], sigma[0]),
+            jnp.where(forward, lead[1], sigma[1]),
+        )
+        first = (get(own, 0, 0), wider(get(own, 0, 1)))
+        first = (first[0], pick(head, plus(sandwich(first[0], start), first[1]), first[1]))
+        swap.wait_recv()
+        total = merged(first, (get(pair, 0), wider(get(pair, 1))))
+        put_map(slots, (pick(head, none, total[0]), total[1]), spot)
+
+    keep(1 - role, whole(downward()[::-1]))
+    for load in loads[2:]:
+        load.wait()
 
     @pl.when(role == 1)
     def _():
         pl.semaphore_wait(met.at[0], 1)
-
-    swap = remote(own.at[1], pair, mate, 0, 0)
-    swap.start()
-    pl.when(role == 0)(total_to(0, True))
-    pl.when(role == 1)(total_to(0, False))
+        advance()
+        pl.semaphore_wait(barrier, receivers(chip) + receivers(chips - 1 - chip))
+        tell(1)
+        for_targets(lambda copy: copy.start())
+        keep(1, whole(upward()))
+        swap.start()
+
+    @pl.when(role == 0)
+    def _():
+        swap.start()
+        keep(0, whole(upward()))
+        advance()
+        pl.semaphore_wait(met.at[1], 1)
+        for_targets(lambda copy: copy.start())
+
     hint = remote(own.at[0], given, mate, 1, 1)
     hint.start()
-
-    for load in loads[2:]:
-        load.wait()
-    forward = role == 0
-    start = (
-        jnp.where(forward, lead[0], sigma[0]),
-        jnp.where(forward, lead[1], sigma[1]),
-    )
-    first = (get(own, 0, 0), wider(get(own, 0, 1)))
-    first = (first[0], pick(head, plus(sandwich(first[0], start), first[1]), first[1]))
-    swap.wait_recv()
-
-    @pl.when(role == 1)
-    def _():
-        pl.semaphore_wait(barrier, receivers(chip) + receivers(chips - 1 - chip))
-        tell(1)
-
-    total = merged(first, (get(pair, 0), wider(get(pair, 1))))
-    total = (pick(head, none, total[0]), total[1])
-    put_map(mine, total)
-
-    @pl.when(role == 0)
-    def _():
-        pl.semaphore_wait(met.at[1], 1)
-
-    def neighbour(d, whole_map):
-        part = pl.ds(0, 3 * width + 16) if whole_map else constant
-        return remote(mine.at[part], slots.at[d - 1, part], me + stride * d, 2 + d, 2 + d)
-
-    def for_kinds(d, sender, act):
-        test = spot + d < group if sender else spot >= d
-        at_head = head if sender else place == d
-        pl.when(jnp.logical_and(test, at_head))(lambda: act(neighbour(d, False)))
-        pl.when(jnp.logical_and(test, jnp.logical_not(at_head)))(lambda: act(neighbour(d, True)))
-
-    for d in reversed(range(1, group)):
-        for_kinds(d, True, lambda copy: copy.start())
 
     g = blocks()[0]
     up, down = upward(), downward()[::-1]
@@ -345,22 +356,33 @@
         put(base, plus(get(base, i), sandwich(factor, get(given, 1))), i)
         put(factors, product(factor, get(given, 0)), 1, i)
 
-    for d in reversed(range(1, group)):
-        for_kinds(d, False, lambda copy: copy.wait_recv())
-    arrived = [get_map(slots, d - 1) for d in reversed(range(1, group))]
-    if arrived:
-        lower = arrived[:-1] and [whole(arrived[:-1])]
-        before = whole(lower + arrived[-1:])
-        total = whole(lower + [merged(arrived[-1], total)])
-    else:
-        before = ((square, zeros), wider(none))
-    before = (pick(head, none, before[0]), pick(head, wider(start), before[1]))
+    for p, test, first in sources():
+        by_kind(test, first, p, spot, lambda copy: copy.wait_recv())
+
+    def group_total():
+        return whole([get_map(slots, p) for p in range(group)])
+
+    start = (
+        jnp.where(forward, lead[0], sigma[0]),
+        jnp.where(forward, lead[1], sigma[1]),
+    )
+
+    def group_before():
+        found = []
+        for p in range(group - 1):
+            m_part, s_part = get_map(slots, p)
+            found.append((pick(p < spot, m_part, (square, zeros)), pick(p < spot, s_part, wider(none))))
+        found = whole(found) if found else ((square, zeros), wider(none))
+        return pick(head, none, found[0]), pick(head, wider(start), found[1])
+
+    if middle:
+        total, before = group_total(), group_before()
 
     def deliveries(k, whole_map):
         part = pl.ds(0, 3 * width + 16) if whole_map else constant
-        at = 2 + group + 2 ** k - 2**near
+        at = 3 + 2**k
         return [
-            remote(relay.at[k - near, part], inbox.at[k - near, part], me + stride * (1 + d), at + d, 2 + group + k - near)
+            remote(relay.at[k - near, part], inbox.at[k - near, part], me + stride * (1 + d), at + d, 3 + group + k - near)
             for d in range(2**k)
         ]
 
@@ -385,21 +407,23 @@
         total = merged(got, total)
         before = merged(got, before)
 
-    last = 2 + group + half - 2**near
-    last_recv = 2 + group + len(middle)
-
-    def final(d, twin):
-        other = me + stride * (1 + d)
-        other = other + 1 - 2 * role if twin else other
-        return remote(post, late, other, last + 2 * d + twin, last_recv)
+    last = 3 + half
+    last_recv = 3 + group + len(middle)
+
+    def final(d, core):
+        other = (me + stride * duo * (1 + d)) // 2 * 2 + core
+        return remote(post, late, other, last + 2 * d + core, last_recv)
 
     @pl.when(gives_last)
     def _():
-        put_packed(post, total[1], 0)
-        for d in reversed(range(half)):
+        value = total if middle else group_total()
+        put_packed(post, value[1], 0)
+        for d in reversed(range(half // duo)):
             final(d, 0).start()
             final(d, 1).start()
 
+    if not middle:
+        before = group_before()
     put(ends, before[0], 0, 0)
     put(ends, before[1], 0, 1)
     share = remote(ends.at[0], ends.at[1], mate, 2, 2)
@@ -430,8 +454,7 @@
     swap.wait_send()
     hint.wait_send()
     share.wait_send()
-    for d in range(1, group):
-        for_kinds(d, True, lambda copy: copy.wait_send())
+    for_targets(lambda copy: copy.wait_send())
     for k in middle:
         for whole_map in (False, True):
 
@@ -442,7 +465,7 @@
 
     @pl.when(gives_last)
     def _():
-        for d in range(half):
+        for d in range(half // duo):
             final(d, 0).wait_send()
             final(d, 1).wait_send()
 
@@ -473,15 +496,14 @@
                 pltpu.VMEM((2, *block), BF),
                 pltpu.VMEM((2, layers, *block), BF),
                 pltpu.VMEM((layers, *block), F32),
-                pltpu.VMEM(chart, BF),
-                pltpu.VMEM((max(group - 1, 1), *chart), BF),
+                pltpu.VMEM((group, *chart), BF),
                 pltpu.VMEM((max(hops, 1), *chart), BF),
                 pltpu.VMEM((max(hops, 1), *chart), BF),
                 pltpu.VMEM((2, 2, *block), BF),
                 pltpu.VMEM(packed, BF),
                 pltpu.VMEM(packed, BF),
-                pltpu.SemaphoreType.DMA((2 + group + half - group + 2 * half,)),
-                pltpu.SemaphoreType.DMA((3 + group + hops,)),
+                pltpu.SemaphoreType.DMA((3 + 3 * half,)),
+                pltpu.SemaphoreType.DMA((4 + group + hops,)),
                 pltpu.SemaphoreType.DMA((4,)),
                 pltpu.SemaphoreType.REGULAR((2,)),
             ],

time: 15.7 us -> 17 us (1.083)
  the two profiles are of different devices: /device:TPU:0 before, /device:TPU:17 now
where the time goes in v3:
time: 17 us; the launch traced here: 16.8 us
  Pallas kernels  16 us (94%)
  local copies, waits for them, and re-layouts  0.8 us (5%)
    pallas_call x1, Pallas kernels, local(): pl.pallas_call(functools.partial(kernel, bits, near), out_shape=jax.Shape...  16 us
    unnamed x1, local copies, waits for them, and re-layouts  0.8 us

profile of v3, /device:TPU:17, one launch (start us, length us, event | category | flops | bytes accessed | tf_op | source)
XLA Modules:
  0.0 16.8 jit_solution(2208748276592483467)
XLA Ops:
  0.0 16.0 %shard_map.46 = f32[2,4,128,128]{3,2,1,0:T(8,128)S(1)} custom-call(bf16[2,4,128,128]{3,2,1,0:T(8,128)(2,1)} %green_hbm.1, bf16[2,4,128,128]{3,2,1,0:T(8,128)(2,1)} %link_hbm.1, bf16[2,128,128]{2,1,0:T(8,128)(2,1)} %lead_hbm.1, bf16[2,128,128]{2,1,0:T(8,128)(2,1)} %sigma_hbm.1), custom_call_target="tpu_custom_call" | custom-call | tf_op jit(solution)/shard_map/pallas_call | solution.py:484
  16.0 0.8 %copy.6 = f32[2,4,128,128]{3,2,1,0:T(8,128)} copy(f32[2,4,128,128]{3,2,1,0:T(8,128)S(1)} %shard_map.46) | data formatting | bytes 1048576

commit v4 on v3

--- a/solution.py
+++ b/solution.py
@@ -82,6 +82,7 @@
     given,
     factors,
     base,
+    mine,
     slots,
     relay,
     inbox,
@@ -106,7 +107,6 @@
     role, chip = me % 2, me // 2
     mate = me + 1 - 2 * role
     chips, half, group = 2**bits, 2 ** (bits - 1), 2**near
-    duo = min(2, group)
     place = chip + role * (chips - 1 - 2 * chip)
     stride = (1 - 2 * role) * 2
     spot = place % group
@@ -115,10 +115,9 @@
     lows = {k: place // 2 ** (k + 1) * 2 ** (k + 1) for k in middle}
     gives = {k: place == lows[k] + 2**k - 1 for k in middle}
     takes = {k: (place // 2**k) % 2 == 1 for k in middle}
-    gives_last = place // duo == half // duo - 1
+    gives_last = place == half - 1
     upper = chip // half
-    there = half - duo + jnp.where(upper == 1, chip, chips - 1 - chip) % duo
-    giver = jnp.where(upper == 1, there, chips - 1 - there) * 2
+    giver = jnp.where(upper == 1, 2 * (half - 1), 2 * half)
     slow = (1 - upper + role) % 2
 
     barrier = pltpu.get_barrier_semaphore()
@@ -130,19 +129,14 @@
         greet(other // 2 * 2 + 1)
 
     def receivers(place):
-        found = group - 1 - place % group + jnp.where(place // duo == half // duo - 1, 2 * (half // duo), 0)
-        if duo > 1:
-            found = found + jnp.where(place % group == group - 1, 1, 0)
+        found = group - 1 - place % group + jnp.where(place == half - 1, 2 * half, 0)
         for k in middle:
             found = found + jnp.where(place % 2 ** (k + 1) == 2**k - 1, 2**k, 0)
         return found
 
     def sources():
-        for p in range(group):
-            test = p < spot
-            if duo > 1 and p == group - 1:
-                test = spot == group - 2
-            yield p, test, place - spot + p == 0
+        for p in reversed(range(group - 1)):
+            yield p, p < spot, place - spot + p == 0
 
     for p, test, _ in sources():
 
@@ -223,7 +217,7 @@
     blank = jnp.zeros((width + 16, width), BF)
     for p, test, first in sources():
 
-        @pl.when(jnp.logical_not(jnp.logical_or(test, spot == p)))
+        @pl.when(jnp.logical_not(test))
         def _():
             put_linear(slots, (square, zeros), p)
             slots[p, constant] = blank
@@ -279,20 +273,16 @@
 
     def neighbour(source, target, whole_map):
         part = pl.ds(0, 3 * width + 16) if whole_map else constant
-        return remote(
-            slots.at[source, part], slots.at[source, part], me + stride * (target - spot), 3 + target, 3 + source
-        )
+        other = me + stride * (target - spot)
+        return remote(mine.at[part], slots.at[source, part], other, 3 + target, 3 + source)
 
     def by_kind(test, first, source, target, act):
         pl.when(jnp.logical_and(test, first))(lambda: act(neighbour(source, target, False)))
         pl.when(jnp.logical_and(test, jnp.logical_not(first)))(lambda: act(neighbour(source, target, True)))
 
     def for_targets(act):
-        for p in reversed(range(group)):
-            test = spot < p
-            if duo > 1 and p == group - 2:
-                test = jnp.logical_or(test, spot == group - 1)
-            by_kind(test, head, spot, p, act)
+        for p in reversed(range(1, group)):
+            by_kind(spot < p, head, spot, p, act)
 
     forward = role == 0
     swap = remote(own.at[1], pair, mate, 0, 0)
@@ -306,7 +296,7 @@
         first = (first[0], pick(head, plus(sandwich(first[0], start), first[1]), first[1]))
         swap.wait_recv()
         total = merged(first, (get(pair, 0), wider(get(pair, 1))))
-        put_map(slots, (pick(head, none, total[0]), total[1]), spot)
+        put_map(mine, (pick(head, none, total[0]), total[1]))
 
     keep(1 - role, whole(downward()[::-1]))
     for load in loads[2:]:
@@ -356,27 +346,21 @@
         put(base, plus(get(base, i), sandwich(factor, get(given, 1))), i)
         put(factors, product(factor, get(given, 0)), 1, i)
 
-    for p, test, first in sources():
-        by_kind(test, first, p, spot, lambda copy: copy.wait_recv())
-
-    def group_total():
-        return whole([get_map(slots, p) for p in range(group)])
-
     start = (
         jnp.where(forward, lead[0], sigma[0]),
         jnp.where(forward, lead[1], sigma[1]),
     )
-
-    def group_before():
-        found = []
-        for p in range(group - 1):
-            m_part, s_part = get_map(slots, p)
-            found.append((pick(p < spot, m_part, (square, zeros)), pick(p < spot, s_part, wider(none))))
-        found = whole(found) if found else ((square, zeros), wider(none))
-        return pick(head, none, found[0]), pick(head, wider(start), found[1])
-
-    if middle:
-        total, before = group_total(), group_before()
+    total, before = get_map(mine), []
+    for p, test, first in sources():
+        by_kind(test, first, p, spot, lambda copy: copy.wait_recv())
+        before.insert(0, get_map(slots, p))
+        if p == group - 2:
+            total = merged(before[0], total)
+    if before[:-1]:
+        lower = whole(before[:-1])
+        total = merged(lower, total)
+        before = [lower, before[-1]]
+    before.append(((square, zeros), wider(none)))
 
     def deliveries(k, whole_map):
         part = pl.ds(0, 3 * width + 16) if whole_map else constant
@@ -386,6 +370,7 @@
             for d in range(2**k)
         ]
 
+    gots = []
     for k in middle:
 
         @pl.when(gives[k])
@@ -403,27 +388,28 @@
             def _():
                 deliveries(k, whole_map)[0].wait_recv()
 
-        got = get_map(inbox, k - near)
-        total = merged(got, total)
-        before = merged(got, before)
+        gots.append(get_map(inbox, k - near))
+        total = merged(gots[-1], total)
 
     last = 3 + half
     last_recv = 3 + group + len(middle)
 
-    def final(d, core):
-        other = (me + stride * duo * (1 + d)) // 2 * 2 + core
-        return remote(post, late, other, last + 2 * d + core, last_recv)
+    def final(order, core):
+        d = order + role * (half - 1 - 2 * order)
+        other = (me + stride * (1 + d)) // 2 * 2 + core
+        return remote(post, late, other, last + 2 * order + core, last_recv)
 
     @pl.when(gives_last)
     def _():
-        value = total if middle else group_total()
-        put_packed(post, value[1], 0)
-        for d in reversed(range(half // duo)):
-            final(d, 0).start()
-            final(d, 1).start()
-
-    if not middle:
-        before = group_before()
+        put_packed(post, total[1], 0)
+        for order in range(half):
+            final(order, 0).start()
+            final(order, 1).start()
+
+    before = whole(before[:2]) if group > 2 else before[0]
+    before = (pick(head, none, before[0]), pick(head, wider(start), before[1]))
+    for got in gots:
+        before = merged(got, before)
     put(ends, before[0], 0, 0)
     put(ends, before[1], 0, 1)
     share = remote(ends.at[0], ends.at[1], mate, 2, 2)
@@ -465,9 +451,9 @@
 
     @pl.when(gives_last)
     def _():
-        for d in range(half // duo):
-            final(d, 0).wait_send()
-            final(d, 1).wait_send()
+        for order in range(half):
+            final(order, 0).wait_send()
+            final(order, 1).wait_send()
 
 
 def solution(mesh):
@@ -496,7 +482,8 @@
                 pltpu.VMEM((2, *block), BF),
                 pltpu.VMEM((2, layers, *block), BF),
                 pltpu.VMEM((layers, *block), F32),
-                pltpu.VMEM((group, *chart), BF),
+                pltpu.VMEM(chart, BF),
+                pltpu.VMEM((max(group - 1, 1), *chart), BF),
                 pltpu.VMEM((max(hops, 1), *chart), BF),
                 pltpu.VMEM((max(hops, 1), *chart), BF),
                 pltpu.VMEM((2, 2, *block), BF),

time: 17 us -> 17.2 us (1.012)
  the two profiles are of different devices: /device:TPU:17 before, /device:TPU:29 now
where the time goes in v4:
time: 17.2 us; the launch traced here: 17.1 us
  Pallas kernels  16.3 us (95%)
  local copies, waits for them, and re-layouts  0.8 us (5%)
    pallas_call x1, Pallas kernels, local(): pl.pallas_call(functools.partial(kernel, bits, near), out_shape=jax.Shape...  16.3 us
    unnamed x1, local copies, waits for them, and re-layouts  0.8 us

profile of v4, /device:TPU:29, one launch (start us, length us, event | category | flops | bytes accessed | tf_op | source)
XLA Modules:
  0.0 17.1 jit_solution(9180449485884962719)
XLA Ops:
  0.0 16.3 %shard_map.46 = f32[2,4,128,128]{3,2,1,0:T(8,128)S(1)} custom-call(bf16[2,4,128,128]{3,2,1,0:T(8,128)(2,1)} %green_hbm.1, bf16[2,4,128,128]{3,2,1,0:T(8,128)(2,1)} %link_hbm.1, bf16[2,128,128]{2,1,0:T(8,128)(2,1)} %lead_hbm.1, bf16[2,128,128]{2,1,0:T(8,128)(2,1)} %sigma_hbm.1), custom_call_target="tpu_custom_call" | custom-call | tf_op jit(solution)/shard_map/pallas_call | solution.py:470
  16.3 0.8 %copy.6 = f32[2,4,128,128]{3,2,1,0:T(8,128)} copy(f32[2,4,128,128]{3,2,1,0:T(8,128)S(1)} %shard_map.46) | data formatting | bytes 1048576

commit v5 on v4

--- a/solution.py
+++ b/solution.py
@@ -298,27 +298,46 @@
         total = merged(first, (get(pair, 0), wider(get(pair, 1))))
         put_map(mine, (pick(head, none, total[0]), total[1]))
 
-    keep(1 - role, whole(downward()[::-1]))
+    def find(at, first):
+        pl.when((upper == 1) == first)(lambda: keep(at, whole(downward()[::-1])))
+        pl.when((upper == 0) == first)(lambda: keep(at, whole(upward())))
+
+    def gather():
+        @pl.when(role == 1)
+        def _():
+            pl.semaphore_wait(barrier, receivers(chip) + receivers(chips - 1 - chip))
+            tell(1)
+
+    def dispatch():
+        @pl.when(role == 0)
+        def _():
+            pl.semaphore_wait(met.at[1], 1)
+
+        for_targets(lambda copy: copy.start())
+
+    find((role + upper) % 2, True)
     for load in loads[2:]:
         load.wait()
 
     @pl.when(role == 1)
     def _():
         pl.semaphore_wait(met.at[0], 1)
+
+    @pl.when(role == upper)
+    def _():
         advance()
-        pl.semaphore_wait(barrier, receivers(chip) + receivers(chips - 1 - chip))
-        tell(1)
-        for_targets(lambda copy: copy.start())
-        keep(1, whole(upward()))
+        gather()
+        dispatch()
+        find(1, False)
         swap.start()
 
-    @pl.when(role == 0)
+    @pl.when(role != upper)
     def _():
         swap.start()
-        keep(0, whole(upward()))
+        find(0, False)
+        gather()
         advance()
-        pl.semaphore_wait(met.at[1], 1)
-        for_targets(lambda copy: copy.start())
+        dispatch()
 
     hint = remote(own.at[0], given, mate, 1, 1)
     hint.start()
@@ -340,12 +359,6 @@
         else:
             put(factors, g[i], 1 - role, i)
             put(base, s_part, i)
-    hint.wait_recv()
-    for i in range(layers):
-        factor = get(factors, 1, i)
-        put(base, plus(get(base, i), sandwich(factor, get(given, 1))), i)
-        put(factors, product(factor, get(given, 0)), 1, i)
-
     start = (
         jnp.where(forward, lead[0], sigma[0]),
         jnp.where(forward, lead[1], sigma[1]),
@@ -353,9 +366,9 @@
     total, before = get_map(mine), []
     for p, test, first in sources():
         by_kind(test, first, p, spot, lambda copy: copy.wait_recv())
-        before.insert(0, get_map(slots, p))
-        if p == group - 2:
-            total = merged(before[0], total)
+    before = [get_map(slots, p) for p in range(group - 1)]
+    if before:
+        total = merged(before[-1], total)
     if before[:-1]:
         lower = whole(before[:-1])
         total = merged(lower, total)
@@ -414,6 +427,11 @@
     put(ends, before[1], 0, 1)
     share = remote(ends.at[0], ends.at[1], mate, 2, 2)
     share.start()
+    hint.wait_recv()
+    for i in range(layers):
+        factor = get(factors, 1, i)
+        put(base, plus(get(base, i), sandwich(factor, get(given, 1))), i)
+        put(factors, product(factor, get(given, 0)), 1, i)
 
     def add(k):
         rows = jnp.concatenate([wide(get(factors, k, i)) for i in range(layers)], axis=0)

time: 17.2 us -> 15.7 us (0.913)
  the two profiles are of different devices: /device:TPU:29 before, /device:TPU:0 now
where the time goes in v5:
time: 15.7 us; the launch traced here: 15.5 us
  Pallas kernels  14.6 us (93%)
  local copies, waits for them, and re-layouts  0.8 us (5%)
    pallas_call x1, Pallas kernels, local(): pl.pallas_call(functools.partial(kernel, bits, near), out_shape=jax.Shape...  14.6 us
    unnamed x1, local copies, waits for them, and re-layouts  0.8 us

profile of v5, /device:TPU:0, one launch (start us, length us, event | category | flops | bytes accessed | tf_op | source)
XLA Modules:
  0.0 15.5 jit_solution(5772223909332611693)
XLA Ops:
  0.0 14.6 %shard_map.46 = f32[2,4,128,128]{3,2,1,0:T(8,128)S(1)} custom-call(bf16[2,4,128,128]{3,2,1,0:T(8,128)(2,1)} %green_hbm.1, bf16[2,4,128,128]{3,2,1,0:T(8,128)(2,1)} %link_hbm.1, bf16[2,128,128]{2,1,0:T(8,128)(2,1)} %lead_hbm.1, bf16[2,128,128]{2,1,0:T(8,128)(2,1)} %sigma_hbm.1), custom_call_target="tpu_custom_call" | custom-call | tf_op jit(solution)/shard_map/pallas_call | solution.py:488
  14.7 0.8 %copy.6 = f32[2,4,128,128]{3,2,1,0:T(8,128)} copy(f32[2,4,128,128]{3,2,1,0:T(8,128)S(1)} %shard_map.46) | data formatting | bytes 1048576

commit v6 on v5

--- a/solution.py
+++ b/solution.py
@@ -407,8 +407,10 @@
     last = 3 + half
     last_recv = 3 + group + len(middle)
 
+    upward_order = [half // 2] + [d for d in range(half) if d != half // 2]
+
     def final(order, core):
-        d = order + role * (half - 1 - 2 * order)
+        d = upward_order[order] + role * (half - 1 - order - upward_order[order])
         other = (me + stride * (1 + d)) // 2 * 2 + core
         return remote(post, late, other, last + 2 * order + core, last_recv)
 

time: 15.7 us -> 16.5 us (1.051)
  the two profiles are of different devices: /device:TPU:0 before, /device:TPU:25 now
where the time goes in v6:
time: 16.5 us; the launch traced here: 16.4 us
  Pallas kernels  15.6 us (95%)
  local copies, waits for them, and re-layouts  0.8 us (5%)
    pallas_call x1, Pallas kernels, local(): pl.pallas_call(functools.partial(kernel, bits, near), out_shape=jax.Shape...  15.6 us
    unnamed x1, local copies, waits for them, and re-layouts  0.8 us

profile of v6, /device:TPU:25, one launch (start us, length us, event | category | flops | bytes accessed | tf_op | source)
XLA Modules:
  0.0 16.4 jit_solution(9743911476708503388)
XLA Ops:
  0.0 15.6 %shard_map.46 = f32[2,4,128,128]{3,2,1,0:T(8,128)S(1)} custom-call(bf16[2,4,128,128]{3,2,1,0:T(8,128)(2,1)} %green_hbm.1, bf16[2,4,128,128]{3,2,1,0:T(8,128)(2,1)} %link_hbm.1, bf16[2,128,128]{2,1,0:T(8,128)(2,1)} %lead_hbm.1, bf16[2,128,128]{2,1,0:T(8,128)(2,1)} %sigma_hbm.1), custom_call_target="tpu_custom_call" | custom-call | tf_op jit(solution)/shard_map/pallas_call | solution.py:490
  15.6 0.8 %copy.6 = f32[2,4,128,128]{3,2,1,0:T(8,128)} copy(f32[2,4,128,128]{3,2,1,0:T(8,128)S(1)} %shard_map.46) | data formatting | bytes 1048576
